TPU v7x, 128 devices: a whole 4x4x4 slice. The times are simulated.
128 devices in a mesh: dp: 4 (over x), fsdp: 32 (over z, y, core).
Axes of the slice: x: 4, y: 4, z: 4, core: 2. Of those that a mesh axis runs over, the one named last changes fastest.
Arguments:
- mlp_input: bfloat16 [1024, 4096], P('dp', 'fsdp'), may hold values from -6 to 6
- residual_in: bfloat16 [1024, 4096], P(('dp', 'fsdp')), may hold values from -6 to 6
- gate_weight: bfloat16 [4096, 14336], P(None, 'fsdp'), may hold values from -0.09375 to 0.09375
- up_weight: bfloat16 [4096, 14336], P(None, 'fsdp'), may hold values from -0.09375 to 0.09375
- down_weight: bfloat16 [14336, 4096], P('fsdp'), may hold values from -0.046875 to 0.046875
- span_index: bfloat16 [65536, 4096], P(('dp', 'fsdp')), may hold values from -6 to 6
- positive_keys: bfloat16 [1024, 4096], P(('dp', 'fsdp')), may hold values from -6 to 6
- request_rows: int32 [128, 128, 8], P(None, ('dp', 'fsdp')), may hold values from 0 to 511, as said below
- request_counts: int32 [128, 128], P(None, ('dp', 'fsdp')), may hold values from 0 to 8, as said below
- negative_slots: int32 [1024, 64], P(('dp', 'fsdp')), may hold values from 0 to 1023, as said below
Outputs:
- query_loss: float32 [1024], P(('dp', 'fsdp'))
- input_grad: bfloat16 [1024, 4096], P('dp', 'fsdp')
- gate_grad: bfloat16 [4096, 14336], P('dp', 'fsdp')
- up_grad: bfloat16 [4096, 14336], P('dp', 'fsdp')
- down_grad: bfloat16 [14336, 4096], P('fsdp', 'dp')
Inputs may be any that keep to these rules, and one draw needn't show every extreme that they name: `request_rows`: entry [r, o, s] is a local row of shard o; it is read only where s < request_counts[r, o]. `request_counts`: for each requesting device r the counts over the 128 shards sum to 512, and some shard gets exactly 8. `negative_slots`: rows q of device r = q // 8; an entry o * 8 + s names slot s of shard o with s < request_counts[r, o]; the 512 entries of a device use each such slot exactly once.
All inputs are finite; a program needn't handle non-finite values.
Results may differ from a plain program's by a relative error of at most 0.017.
Values may be sent and summed in bfloat16 or wider, within the bound.
A program may use at most 128 MiB of HBM per device.

v0:
```python
import jax
import jax.numpy as jnp
from jax import lax
from jax.sharding import PartitionSpec as P

inverse_temp = 50.0
eps = 1e-06
contract_first = (((0,), (0,)), ((), ()))
contract_last = (((1,), (1,)), ((), ()))


def silu_grad(gate_act):
    sigmoid_gate = jax.nn.sigmoid(gate_act)
    return sigmoid_gate * (1.0 + gate_act * (1.0 - sigmoid_gate))


def contrast(unit_rows, row_norm, key_block):
    key_unit = key_block / jnp.sqrt(jnp.sum(key_block * key_block, axis=-1, keepdims=True) + eps)
    scores = inverse_temp * jnp.einsum(
        "qd,qnd->qn", unit_rows, key_unit, precision=lax.Precision.HIGHEST
    )
    weights = jnp.exp(scores)
    exp_total = jnp.sum(weights, axis=-1)
    query_loss = jnp.log(exp_total) - scores[:, 0]
    column = lax.broadcasted_iota(jnp.int32, scores.shape, 1)
    coeffs = weights / exp_total[:, None] - (column == 0).astype(scores.dtype)
    pull_term = inverse_temp * jnp.einsum(
        "qn,qnd->qd", coeffs, key_unit, precision=lax.Precision.HIGHEST
    )
    inner_term = jnp.sum(coeffs * scores, axis=-1)
    head_grad = ((pull_term - inner_term[:, None] * unit_rows) / row_norm[:, None]).astype(
        jnp.bfloat16
    )
    return (query_loss, head_grad)


def shards(
    mlp_input,
    residual_in,
    gate_weight,
    up_weight,
    down_weight,
    span_index,
    positive_keys,
    request_rows,
    request_counts,
    negative_slots,
):
    dp_count = lax.axis_size("dp")
    fsdp_count = lax.axis_size("fsdp")
    owners = dp_count * fsdp_count
    slot_cap = request_rows.shape[2]
    feature_width = span_index.shape[1]
    whole_input = lax.all_gather(mlp_input, "fsdp", axis=1, tiled=True)
    gate_act = jnp.dot(whole_input, gate_weight, preferred_element_type=jnp.float32)
    up_act = jnp.dot(whole_input, up_weight, preferred_element_type=jnp.float32)
    hidden = (jax.nn.silu(gate_act) * up_act).astype(jnp.bfloat16)
    branch = lax.psum_scatter(
        jnp.dot(hidden, down_weight, preferred_element_type=jnp.float32).astype(jnp.bfloat16),
        "fsdp",
        scatter_dimension=0,
        tiled=True,
    ).astype(jnp.float32)
    top_state = branch + residual_in.astype(jnp.float32)
    row_norm = jnp.sqrt(jnp.sum(top_state * top_state, axis=-1) + eps)
    unit_rows = top_state / row_norm[:, None]
    row_table = request_rows[:, 0, :]
    count_table = request_counts[:, 0]
    picked = jnp.take(span_index, row_table.reshape(-1), axis=0).reshape(
        owners, slot_cap, feature_width
    )
    live_mask = lax.broadcasted_iota(jnp.int32, (owners, slot_cap), 1) < count_table[:, None]
    picked = jnp.where(live_mask[..., None], picked, jnp.zeros_like(picked))
    buffer = lax.all_to_all(picked, ("dp", "fsdp"), split_axis=0, concat_axis=0, tiled=True)
    flat_buffer = buffer.reshape(owners * slot_cap, feature_width)
    fetched = jnp.take(flat_buffer, negative_slots.reshape(-1), axis=0)
    fetched = fetched.reshape(
        negative_slots.shape[0], negative_slots.shape[1], feature_width
    ).astype(jnp.float32)
    key_block = jnp.concatenate([positive_keys.astype(jnp.float32)[:, None, :], fetched], axis=1)
    query_loss, head_grad = contrast(unit_rows, row_norm, key_block)
    gathered_grad = lax.all_gather(head_grad, "fsdp", axis=0, tiled=True)
    hidden_grad = lax.dot_general(
        gathered_grad, down_weight, contract_last, preferred_element_type=jnp.float32
    )
    gate_grad_act = (hidden_grad * up_act * silu_grad(gate_act)).astype(jnp.bfloat16)
    up_grad_act = (hidden_grad * jax.nn.silu(gate_act)).astype(jnp.bfloat16)
    input_term = lax.dot_general(
        gate_grad_act, gate_weight, contract_last, preferred_element_type=jnp.float32
    ) + lax.dot_general(up_grad_act, up_weight, contract_last, preferred_element_type=jnp.float32)
    input_grad = lax.psum_scatter(
        input_term.astype(jnp.bfloat16), "fsdp", scatter_dimension=1, tiled=True
    )
    gate_term = lax.dot_general(
        whole_input, gate_grad_act, contract_first, preferred_element_type=jnp.float32
    )
    up_term = lax.dot_general(
        whole_input, up_grad_act, contract_first, preferred_element_type=jnp.float32
    )
    down_term = lax.dot_general(
        hidden, gathered_grad, contract_first, preferred_element_type=jnp.float32
    )
    gate_sum, up_sum = (
        lax.psum_scatter(
            gate_term.astype(jnp.bfloat16), "dp", scatter_dimension=0, tiled=True
        ).astype(jnp.float32),
        lax.psum_scatter(
            up_term.astype(jnp.bfloat16), "dp", scatter_dimension=0, tiled=True
        ).astype(jnp.float32),
    )
    down_sum = lax.psum_scatter(
        down_term.astype(jnp.bfloat16), "dp", scatter_dimension=1, tiled=True
    )
    gate_grad = gate_sum.astype(jnp.bfloat16)
    up_grad = up_sum.astype(jnp.bfloat16)
    return (query_loss, input_grad, gate_grad, up_grad, down_sum)


def solution(mesh):
    return jax.shard_map(
        shards,
        mesh=mesh,
        in_specs=(
            P("dp", "fsdp"),
            P(("dp", "fsdp"), None),
            P(None, "fsdp"),
            P(None, "fsdp"),
            P("fsdp", None),
            P(("dp", "fsdp"), None),
            P(("dp", "fsdp"), None),
            P(None, ("dp", "fsdp"), None),
            P(None, ("dp", "fsdp")),
            P(("dp", "fsdp"), None),
        ),
        out_specs=(
            P(("dp", "fsdp")),
            P("dp", "fsdp"),
            P("dp", "fsdp"),
            P("dp", "fsdp"),
            P("fsdp", "dp"),
        ),
        check_vma=False,
    )
```

profile of v0, /device:TPU:1, one launch (start us, length us, event | category | flops | bytes accessed | tf_op | source)
XLA Modules:
  0.0 547.2 jit_solution(9983815885430911765)
XLA Ops:
  7.2 0.7 all-gather.3.cloned.1.call-update
  7.9 0.8 copy.21
  8.7 0.1 reshape_squeeze.6
  8.8 0.7 iota_compare_fusion
  9.6 0.7 compare_and_fusion
  10.3 0.1 copy.20
  10.4 17.8 %gather_fusion = bf16[1024,4096]{1,0:T(8,128)(2,1)} fusion(bf16[512,4096]{1,0:T(8,128)(2,1)} %param.15, s32[1024]{0:T(1024)S(1)} %broadcast_clamp_fusion), kind=kCustom, calls=%fused_computation | custom fusion | bytes 16781312 | tf_op jit(solution)/shard_map/jit(_take)/gather | solution.py:69
  28.2 7.4 %fusion.1 = bf16[128,8,4096]{2,1,0:T(8,128)(2,1)} fusion(bf16[1024,4096]{1,0:T(8,128)(2,1)} %gather_fusion, pred[128,8]{1,0:T(8,128)(4,1)S(1)} %copy.20, pred[128,8]{1,0:T(8,128)(4,1)S(1)} %iota_compare_fusion), kind=kLoop, calls=%fused_computation.6 | loop fusion | flops 8388608 | bytes 16779264 | tf_op jit(solution)/shard_map/jit(_where)/select_n | solution.py:73
  35.6 11.9 %all-to-all-start = ((bf16[128,8,4096]{2,1,0:T(8,128)(2,1)}), bf16[128,8,4096]{2,1,0:T(8,128)(2,1)}, u32[]{:S(2)}, u32[]{:S(2)}) async-start(bf16[128,8,4096]{2,1,0:T(8,128)(2,1)} %fusion.1), calls=%async_computation.1 | async-start | bytes 16777216 | tf_op jit(solution)/shard_map/all_to_all | solution.py:74
  47.6 94.3 %all-gather.3.cloned.1.call-done = bf16[256,4096]{1,0:T(8,128)(2,1)} async-done(((bf16[256,128]{1,0:T(8,128)(2,1)}), bf16[256,4096]{1,0:T(8,128)(2,1)}) %all-gather.3.cloned.1.call-update) | async-done | bytes 2097168 | tf_op jit(solution)/shard_map/all_gather | solution.py:54
  141.9 4.0 fusion.20
  145.9 0.4 copy-done.4
  146.3 1.9 multiply_convert_fusion.2
  148.3 0.1 copy-done.3
  148.4 2.6 convolution_convert_fusion.3
  151.0 0.2 all-gather.5.cloned.1.call-start
  151.3 0.1 reshape.130
  151.3 0.1 copy.22
  151.5 80.2 %reduce-scatter.8.cloned.1.call-done = bf16[8,4096]{1,0:T(8,128)(2,1)} async-done(((bf16[256,4096]{1,0:T(8,128)(2,1)}), bf16[8,4096]{1,0:T(8,128)(2,1)}) %reduce-scatter.8.cloned.1.call-update) | async-done | bytes 65552 | tf_op jit(solution)/shard_map/reduce_scatter | solution.py:58
  231.7 1.0 multiply_reduce_fusion
  232.7 0.9 fusion.16
  233.6 13.1 %gather_fusion.1 = bf16[512,4096]{1,0:T(8,128)(2,1)} fusion(bf16[1024,4096]{1,0:T(8,128)(2,1)} %bitcast.6, s32[1024]{0:T(1024)S(1)} %pad_clamp_fusion), kind=kCustom, calls=%fused_computation.1 | custom fusion | bytes 8390656 | tf_op jit(solution)/shard_map/jit(_take)/gather | solution.py:76
  246.7 2.6 broadcast_select_fusion
  249.3 2.2 fusion
  251.5 8.5 %fusion.3 = f32[8,1,65]{2,1,0:T(1,128)S(1)} fusion(f32[8,65]{1,0:T(8,128)S(1)} %add_sqrt_fusion, bf16[8,64,4096]{2,1,0:T(8,128)(2,1)S(1)} %broadcast_select_fusion, bf16[8,1,4096]{2,1,0:T(2,128)(2,1)S(1)} %copy.22, f32[8,4096,1]{1,0,2:T(8,128)S(1)} %fusion.16), kind=kOutput, calls=%fused_computation.8 | convolution fusion | flops 36208640 | bytes 4395072 | tf_op jit(solution)/shard_map/qd,qnd->qn/dot_general | solution.py:19
  260.0 0.1 copy.24
  260.2 0.1 multiply_reduce_fusion.1
  260.3 0.1 copy.25
  260.3 7.8 %fusion.2 = f32[8,1,4096]{2,1,0:T(1,128)S(1)} fusion(f32[8,65,1]{1,2,0:T(1,128)S(1)} %copy.25, f32[8,65]{1,0:T(8,128)S(1)} %add_sqrt_fusion, bf16[8,64,4096]{2,1,0:T(8,128)(2,1)} %copy-done, bf16[8,1,4096]{2,1,0:T(2,128)(2,1)S(1)} %copy.22), kind=kOutput, calls=%fused_computation.7 | convolution fusion | flops 36208640 | bytes 4395072 | tf_op jit(solution)/shard_map/qn,qnd->qd/dot_general | solution.py:27
  268.2 0.7 fusion.12
  269.0 45.4 %all-gather.5.cloned.1.call-done = bf16[256,4096]{1,0:T(8,128)(2,1)} async-done(((bf16[8,4096]{1,0:T(8,128)(2,1)}), bf16[256,4096]{1,0:T(8,128)(2,1)}) %all-gather.5.cloned.1.call-update) | async-done | bytes 2097168 | tf_op jit(solution)/shard_map/all_gather | solution.py:82
  314.3 4.1 multiply_convert_fusion
  318.5 1.3 fusion.21
  319.8 0.7 copy-done.5
  320.5 2.7 fusion.6
  323.2 4.1 copy.27
  327.4 2.9 fusion.4
  330.3 0.0 reduce-scatter.12.cloned.1.call-start
  330.4 2.9 fusion.5
  333.3 0.0 reduce-scatter.14.cloned.1.call-start
  333.4 1.5 copy-done.6
  334.9 3.0 convolution_convert_fusion
  338.0 0.5 fusion.17
  338.5 65.1 %reduce-scatter.16.cloned.1.call-done = bf16[128,256]{1,0:T(8,128)(2,1)} async-done(((bf16[4096,256]{1,0:T(8,128)(2,1)}), bf16[128,256]{1,0:T(8,128)(2,1)}) %reduce-scatter.16.cloned.1.call-update) | async-done | bytes 65552
  403.6 1.6 copy.28
  405.2 44.7 %reduce-scatter.10.cloned.1.call-done = bf16[1024,448]{0,1:T(8,128)(2,1)} async-done(((bf16[4096,448]{0,1:T(8,128)(2,1)}), bf16[1024,448]{0,1:T(8,128)(2,1)}) %reduce-scatter.10.cloned.1.call-update) | async-done | bytes 917520 | tf_op jit(solution)/shard_map/reduce_scatter | solution.py:104
  449.9 45.1 %reduce-scatter.12.cloned.1.call-done = bf16[1024,448]{0,1:T(8,128)(2,1)} async-done(((bf16[4096,448]{0,1:T(8,128)(2,1)}), bf16[1024,448]{0,1:T(8,128)(2,1)}) %reduce-scatter.12.cloned.1.call-update) | async-done | bytes 917520 | tf_op jit(solution)/shard_map/reduce_scatter | solution.py:107
  495.1 45.3 %reduce-scatter.14.cloned.1.call-done = bf16[448,1024]{1,0:T(8,128)(2,1)} async-done(((bf16[448,4096]{1,0:T(8,128)(2,1)}), bf16[448,1024]{1,0:T(8,128)(2,1)}) %reduce-scatter.14.cloned.1.call-update) | async-done | bytes 917520 | tf_op jit(solution)/shard_map/reduce_scatter | solution.py:111
  (38 shorter events, 0.4 us)
Async XLA Ops:
  7.2 134.8 %all-gather.3.cloned.1.call-start = ((), (), s32[]{:S(2)}) async-start(), calls=%async_computation.6 | async-start | bytes 2162688 | tf_op jit(solution)/shard_map/all_gather | solution.py:54
  35.6 198.0 %all-to-all-start = ((bf16[128,8,4096]{2,1,0:T(8,128)(2,1)}), bf16[128,8,4096]{2,1,0:T(8,128)(2,1)}, u32[]{:S(2)}, u32[]{:S(2)}) async-start(bf16[128,8,4096]{2,1,0:T(8,128)(2,1)} %fusion.1), calls=%async_computation.1 | async-start | bytes 16777216 | tf_op jit(solution)/shard_map/all_to_all | solution.py:74
  47.6 184.1 %reduce-scatter.8.cloned.1.call-start = ((), (), s32[]{:S(2)}) async-start(), calls=%async_computation.7 | async-start | bytes 2162688 | tf_op jit(solution)/shard_map/reduce_scatter | solution.py:58
  141.9 4.0 copy-start.1
  141.9 4.4 copy-start.4
  146.3 2.0 copy-start.3
  148.3 3.0 copy-start.10
  148.3 3.1 copy-start.9
  148.3 83.4 %copy-start.7 = (bf16[8,4096]{1,0:T(8,128)(2,1)S(1)}, bf16[8,4096]{1,0:T(8,128)(2,1)}, u32[]{:S(2)}) copy-start(bf16[8,4096]{1,0:T(8,128)(2,1)} %param.11) | copy-start | bytes 196612
  151.0 163.3 %all-gather.5.cloned.1.call-start = ((), (), s32[]{:S(2)}) async-start(), calls=%async_computation.8 | async-start | bytes 2162688 | tf_op jit(solution)/shard_map/all_gather | solution.py:82
  249.3 2.2 copy-start
  260.3 7.8 %copy-start.8 = (bf16[8,4096]{1,0:T(8,128)(2,1)S(1)}, bf16[8,4096]{1,0:T(8,128)(2,1)}, u32[]{:S(2)}) copy-start(bf16[8,4096]{1,0:T(8,128)(2,1)} %reduce-scatter.8.cloned.1.call-done) | copy-start | bytes 196612
  268.9 134.7 %reduce-scatter.16.cloned.1.call-start = ((), (), s32[]{:S(2)}) async-start(), calls=%async_computation.12 | async-start | bytes 2162688
  314.3 4.1 copy-start.2
  318.4 2.0 copy-start.5
  327.3 122.6 %reduce-scatter.10.cloned.1.call-start = ((), (), s32[]{:S(2)}) async-start(), calls=%async_computation.9 | async-start | bytes 4587520 | tf_op jit(solution)/shard_map/reduce_scatter | solution.py:104
  330.3 164.7 %reduce-scatter.12.cloned.1.call-start = ((), (), s32[]{:S(2)}) async-start(), calls=%async_computation.10 | async-start | bytes 4587520 | tf_op jit(solution)/shard_map/reduce_scatter | solution.py:107
  333.3 1.6 copy-start.6
  333.3 207.0 %reduce-scatter.14.cloned.1.call-start = ((), (), s32[]{:S(2)}) async-start(), calls=%async_computation.11 | async-start | bytes 4587520 | tf_op jit(solution)/shard_map/reduce_scatter | solution.py:111
Sparse Core Ops, SparseCore 0:
  10.2 131.7 all-gather.2
  151.1 80.5 reduce-scatter.7
  269.1 45.2 all-gather.4
  327.4 76.1 reduce-scatter.15
  406.5 43.4 reduce-scatter.9
  452.8 42.2 reduce-scatter.11
  498.0 42.2 reduce-scatter.13
where the time goes:
time: 548 us; the launch traced here: 547 us
  waiting for transfers between devices  421 us (77%)
  matrix products  41.9 us (8%)
  local copies, waits for them, and re-layouts  40.7 us (7%)
  other arithmetic  17 us (3%)
  between operations  14.3 us (3%)
  starting transfers between devices  12.4 us (2%)
    all_gather x1, waiting for transfers between devices, shards(): whole_input = lax.all_gather(mlp_input, 'fsdp', axis=1, tiled=True)  94.3 us
    reduce_scatter x1, waiting for transfers between devices, shards(): lax.psum_scatter(jnp.dot(hidden, down_weight, preferred_element_type=jnp....  80.2 us
    unnamed x8, waiting for transfers between devices  65.9 us
    all_gather x1, waiting for transfers between devices, shards(): gathered_grad = lax.all_gather(head_grad, 'fsdp', axis=0, tiled=True)  45.4 us
    reduce_scatter x1, waiting for transfers between devices, shards(): lax.psum_scatter(down_term.astype(jnp.bfloat16), 'dp', scatter_dimension=...  45.3 us
    reduce_scatter x1, waiting for transfers between devices, shards(): lax.psum_scatter(up_term.astype(jnp.bfloat16), 'dp', scatter_dimension=0,...  45.1 us
    reduce_scatter x1, waiting for transfers between devices, shards(): lax.psum_scatter(gate_term.astype(jnp.bfloat16), 'dp', scatter_dimension=...  44.7 us
    gather x1, local copies, waits for them, and re-layouts, shards(): jnp.take(span_index, row_table.reshape(-1), axis=0)  17.8 us
  transfers between devices with their start and end apart: 8, of which 7 were waited for; matrix products, arithmetic and copies ran while one was open for 9% of the time, Pallas kernels for 0%

commit v1 on v0

--- a/solution.py
+++ b/solution.py
@@ -51,7 +51,9 @@
     owners = dp_count * fsdp_count
     slot_cap = request_rows.shape[2]
     feature_width = span_index.shape[1]
-    whole_input = lax.all_gather(mlp_input, "fsdp", axis=1, tiled=True)
+    whole_input = jnp.concatenate(
+        lax.all_to_all(jnp.stack([mlp_input] * lax.axis_size("fsdp")), "fsdp", 0, 0), axis=1
+    )
     gate_act = jnp.dot(whole_input, gate_weight, preferred_element_type=jnp.float32)
     up_act = jnp.dot(whole_input, up_weight, preferred_element_type=jnp.float32)
     hidden = (jax.nn.silu(gate_act) * up_act).astype(jnp.bfloat16)

time: 548 us -> 496 us (0.905)
  waiting for transfers between devices: 421 us -> 364 us
    all_gather x1 -> x0, waiting for transfers between devices: 94.3 us -> none  [shards(): whole_input = lax.all_gather(mlp_input, 'fsdp', axis=1, tiled=True)]
    reduce_scatter x1, waiting for transfers between devices: 80.2 us -> 116 us  [shards(): lax.psum_scatter(jnp.dot(hidden, down_weight, preferred_element_type=jnp....]
    all_to_all x0 -> x1, starting transfers between devices: none -> 9.6 us  [shards(): lax.all_to_all(jnp.stack([mlp_input] * lax.axis_size('fsdp')), 'fsdp', 0, 0)]
    unnamed x8 -> x7, waiting for transfers between devices: 65.9 us -> 65.2 us
where the time goes in v1:
time: 496 us; the launch traced here: 495 us
  waiting for transfers between devices  364 us (73%)
  local copies, waits for them, and re-layouts  42.1 us (8%)
  matrix products  41.3 us (8%)
  starting transfers between devices  17.6 us (4%)
  other arithmetic  15.7 us (3%)
  between operations  14.4 us (3%)
    reduce_scatter x1, waiting for transfers between devices, shards(): lax.psum_scatter(jnp.dot(hidden, down_weight, preferred_element_type=jnp....  116 us
    unnamed x7, waiting for transfers between devices  65.2 us
    all_gather x1, waiting for transfers between devices, shards(): gathered_grad = lax.all_gather(head_grad, 'fsdp', axis=0, tiled=True)  45.3 us
    reduce_scatter x1, waiting for transfers between devices, shards(): lax.psum_scatter(down_term.astype(jnp.bfloat16), 'dp', scatter_dimension=...  45.1 us
    reduce_scatter x1, waiting for transfers between devices, shards(): lax.psum_scatter(up_term.astype(jnp.bfloat16), 'dp', scatter_dimension=0,...  45.1 us
    reduce_scatter x1, waiting for transfers between devices, shards(): lax.psum_scatter(gate_term.astype(jnp.bfloat16), 'dp', scatter_dimension=...  44.7 us
    gather x1, local copies, waits for them, and re-layouts, shards(): jnp.take(span_index, row_table.reshape(-1), axis=0)  17.8 us
    gather x1, local copies, waits for them, and re-layouts, shards(): fetched = jnp.take(flat_buffer, negative_slots.reshape(-1), axis=0)  13 us
  transfers between devices with their start and end apart: 8, of which 7 were waited for; matrix products, arithmetic and copies ran while one was open for 9% of the time, Pallas kernels for 0%

profile of v1, /device:TPU:1, one launch (start us, length us, event | category | flops | bytes accessed | tf_op | source)
XLA Modules:
  0.0 495.0 jit_solution(11528737958282596286)
XLA Ops:
  7.2 0.9 copy.21
  8.1 1.6 stack.2
  9.7 9.6 %all-to-all-start = ((bf16[32,256,128]{1,2,0:T(8,128)(2,1)}), bf16[32,256,128]{1,2,0:T(8,128)(2,1)S(1)}, u32[]{:S(2)}, u32[]{:S(2)}) async-start(bf16[32,256,128]{1,2,0:T(8,128)(2,1)} %stack.2), calls=%async_computation | async-start | bytes 4194304 | tf_op jit(solution)/shard_map/all_to_all | solution.py:55
  19.3 0.1 copy.23
  19.4 0.1 reshape_squeeze.6
  19.5 0.1 copy.22
  19.7 17.8 %gather_fusion = bf16[1024,4096]{1,0:T(8,128)(2,1)} fusion(bf16[512,4096]{1,0:T(8,128)(2,1)} %param.15, s32[1024]{0:T(1024)S(1)} %broadcast_clamp_fusion), kind=kCustom, calls=%fused_computation | custom fusion | bytes 16781312 | tf_op jit(solution)/shard_map/jit(_take)/gather | solution.py:71
  37.5 0.1 iota_compare_fusion
  37.6 7.4 %fusion.1 = bf16[128,8,4096]{2,1,0:T(8,128)(2,1)} fusion(bf16[1024,4096]{1,0:T(8,128)(2,1)} %gather_fusion, pred[128,8]{1,0:T(8,128)(4,1)S(1)} %copy.22, pred[128,8]{1,0:T(8,128)(4,1)S(1)} %iota_compare_fusion), kind=kLoop, calls=%fused_computation.6 | loop fusion | flops 8388608 | bytes 16779264 | tf_op jit(solution)/shard_map/jit(_where)/select_n | solution.py:75
  45.0 2.1 all-to-all-done
  47.1 7.6 %all-to-all-start.1 = ((bf16[128,8,4096]{2,1,0:T(8,128)(2,1)}), bf16[128,8,4096]{2,1,0:T(8,128)(2,1)}, u32[]{:S(2)}, u32[]{:S(2)}) async-start(bf16[128,8,4096]{2,1,0:T(8,128)(2,1)} %fusion.1), calls=%async_computation.2 | async-start | bytes 16777216 | tf_op jit(solution)/shard_map/all_to_all | solution.py:76
  54.8 3.3 fusion.21
  58.2 1.9 multiply_convert_fusion.2
  60.1 0.1 copy-done.2
  60.2 2.6 convolution_convert_fusion.3
  62.8 0.2 all-gather.2.cloned.1.call-start
  63.1 0.1 reshape.140
  63.2 0.1 copy.24
  63.3 116.4 %reduce-scatter.8.cloned.1.call-done = bf16[8,4096]{1,0:T(8,128)(2,1)} async-done(((bf16[256,4096]{1,0:T(8,128)(2,1)}), bf16[8,4096]{1,0:T(8,128)(2,1)}) %reduce-scatter.8.cloned.1.call-update) | async-done | bytes 65552 | tf_op jit(solution)/shard_map/reduce_scatter | solution.py:60
  179.7 1.0 multiply_reduce_fusion
  180.7 0.9 fusion.16
  181.6 13.0 %gather_fusion.1 = bf16[512,4096]{1,0:T(8,128)(2,1)} fusion(bf16[1024,4096]{1,0:T(8,128)(2,1)} %bitcast.9, s32[1024]{0:T(1024)S(1)} %pad_clamp_fusion), kind=kCustom, calls=%fused_computation.1 | custom fusion | bytes 8390656 | tf_op jit(solution)/shard_map/jit(_take)/gather | solution.py:78
  194.7 2.6 broadcast_select_fusion
  197.3 2.2 fusion
  199.5 8.5 %fusion.3 = f32[8,1,65]{2,1,0:T(1,128)S(1)} fusion(f32[8,65]{1,0:T(8,128)S(1)} %add_sqrt_fusion, bf16[8,64,4096]{2,1,0:T(8,128)(2,1)S(1)} %broadcast_select_fusion, bf16[8,1,4096]{2,1,0:T(2,128)(2,1)S(1)} %copy.24, f32[8,4096,1]{1,0,2:T(8,128)S(1)} %fusion.16), kind=kOutput, calls=%fused_computation.8 | convolution fusion | flops 36208640 | bytes 4395072 | tf_op jit(solution)/shard_map/qd,qnd->qn/dot_general | solution.py:19
  208.0 0.1 copy.26
  208.2 0.1 multiply_reduce_fusion.1
  208.3 0.1 copy.27
  208.3 7.8 %fusion.2 = f32[8,1,4096]{2,1,0:T(1,128)S(1)} fusion(f32[8,65,1]{1,2,0:T(1,128)S(1)} %copy.27, f32[8,65]{1,0:T(8,128)S(1)} %add_sqrt_fusion, bf16[8,64,4096]{2,1,0:T(8,128)(2,1)} %copy-done, bf16[8,1,4096]{2,1,0:T(2,128)(2,1)S(1)} %copy.24), kind=kOutput, calls=%fused_computation.7 | convolution fusion | flops 36208640 | bytes 4395072 | tf_op jit(solution)/shard_map/qn,qnd->qd/dot_general | solution.py:27
  216.2 0.7 fusion.12
  217.0 45.3 %all-gather.2.cloned.1.call-done = bf16[256,4096]{1,0:T(8,128)(2,1)} async-done(((bf16[8,4096]{1,0:T(8,128)(2,1)}), bf16[256,4096]{1,0:T(8,128)(2,1)}) %all-gather.2.cloned.1.call-update) | async-done | bytes 2097168 | tf_op jit(solution)/shard_map/all_gather | solution.py:84
  262.3 4.1 multiply_convert_fusion
  266.4 1.3 fusion.20
  267.7 0.7 copy-done.4
  268.5 2.7 fusion.6
  271.2 4.1 copy.29
  275.3 3.0 fusion.4
  278.3 0.0 reduce-scatter.12.cloned.1.call-start
  278.4 3.0 fusion.5
  281.4 0.0 reduce-scatter.14.cloned.1.call-start
  281.4 1.6 copy-done.5
  283.0 3.0 convolution_convert_fusion
  286.0 0.5 fusion.17
  286.6 65.1 %reduce-scatter.16.cloned.1.call-done = bf16[128,256]{1,0:T(8,128)(2,1)} async-done(((bf16[4096,256]{1,0:T(8,128)(2,1)}), bf16[128,256]{1,0:T(8,128)(2,1)}) %reduce-scatter.16.cloned.1.call-update) | async-done | bytes 65552
  351.6 1.6 copy.30
  353.2 44.7 %reduce-scatter.10.cloned.1.call-done = bf16[1024,448]{0,1:T(8,128)(2,1)} async-done(((bf16[4096,448]{0,1:T(8,128)(2,1)}), bf16[1024,448]{0,1:T(8,128)(2,1)}) %reduce-scatter.10.cloned.1.call-update) | async-done | bytes 917520 | tf_op jit(solution)/shard_map/reduce_scatter | solution.py:106
  397.9 45.1 %reduce-scatter.12.cloned.1.call-done = bf16[1024,448]{0,1:T(8,128)(2,1)} async-done(((bf16[4096,448]{0,1:T(8,128)(2,1)}), bf16[1024,448]{0,1:T(8,128)(2,1)}) %reduce-scatter.12.cloned.1.call-update) | async-done | bytes 917520 | tf_op jit(solution)/shard_map/reduce_scatter | solution.py:109
  443.0 45.1 %reduce-scatter.14.cloned.1.call-done = bf16[448,1024]{1,0:T(8,128)(2,1)} async-done(((bf16[448,4096]{1,0:T(8,128)(2,1)}), bf16[448,1024]{1,0:T(8,128)(2,1)}) %reduce-scatter.14.cloned.1.call-update) | async-done | bytes 917520 | tf_op jit(solution)/shard_map/reduce_scatter | solution.py:113
  (41 shorter events, 0.4 us)
Async XLA Ops:
  7.2 12.1 %copy-start.9 = (s32[128,1,8]{0,2,1:T(8,128)S(1)}, s32[128,1,8]{0,2,1:T(8,128)}, u32[]{:S(2)}) copy-start(s32[128,1,8]{0,2,1:T(8,128)} %param.17) | copy-start | bytes 12292
  9.7 37.5 %all-to-all-start = ((bf16[32,256,128]{1,2,0:T(8,128)(2,1)}), bf16[32,256,128]{1,2,0:T(8,128)(2,1)S(1)}, u32[]{:S(2)}, u32[]{:S(2)}) async-start(bf16[32,256,128]{1,2,0:T(8,128)(2,1)} %stack.2), calls=%async_computation | async-start | bytes 4194304 | tf_op jit(solution)/shard_map/all_to_all | solution.py:55
  19.7 17.8 %copy-start.11 = (s32[128,1]{0,1:T(1,128)S(1)}, s32[128,1]{0,1:T(1,128)}, u32[]{:S(2)}) copy-start(s32[128,1]{0,1:T(1,128)} %param.18) | copy-start | bytes 1540
  47.1 134.5 %all-to-all-start.1 = ((bf16[128,8,4096]{2,1,0:T(8,128)(2,1)}), bf16[128,8,4096]{2,1,0:T(8,128)(2,1)}, u32[]{:S(2)}, u32[]{:S(2)}) async-start(bf16[128,8,4096]{2,1,0:T(8,128)(2,1)} %fusion.1), calls=%async_computation.2 | async-start | bytes 16777216 | tf_op jit(solution)/shard_map/all_to_all | solution.py:76
  54.8 124.9 %reduce-scatter.8.cloned.1.call-start = ((), (), s32[]{:S(2)}) async-start(), calls=%async_computation.7 | async-start | bytes 2162688 | tf_op jit(solution)/shard_map/reduce_scatter | solution.py:60
  54.8 3.3 copy-start.3
  58.1 2.0 copy-start.2
  60.1 3.0 copy-start.10
  60.1 3.1 copy-start.8
  60.1 119.6 %copy-start.6 = (bf16[8,4096]{1,0:T(8,128)(2,1)S(1)}, bf16[8,4096]{1,0:T(8,128)(2,1)}, u32[]{:S(2)}) copy-start(bf16[8,4096]{1,0:T(8,128)(2,1)} %param.11) | copy-start | bytes 196612
  62.8 199.5 %all-gather.2.cloned.1.call-start = ((), (), s32[]{:S(2)}) async-start(), calls=%async_computation.8 | async-start | bytes 2162688 | tf_op jit(solution)/shard_map/all_gather | solution.py:84
  197.3 2.2 copy-start
  208.3 7.8 %copy-start.7 = (bf16[8,4096]{1,0:T(8,128)(2,1)S(1)}, bf16[8,4096]{1,0:T(8,128)(2,1)}, u32[]{:S(2)}) copy-start(bf16[8,4096]{1,0:T(8,128)(2,1)} %reduce-scatter.8.cloned.1.call-done) | copy-start | bytes 196612
  216.9 134.7 %reduce-scatter.16.cloned.1.call-start = ((), (), s32[]{:S(2)}) async-start(), calls=%async_computation.12 | async-start | bytes 2162688
  262.3 4.1 copy-start.1
  266.4 2.0 copy-start.4
  275.3 122.6 %reduce-scatter.10.cloned.1.call-start = ((), (), s32[]{:S(2)}) async-start(), calls=%async_computation.9 | async-start | bytes 4587520 | tf_op jit(solution)/shard_map/reduce_scatter | solution.py:106
  278.3 164.7 %reduce-scatter.12.cloned.1.call-start = ((), (), s32[]{:S(2)}) async-start(), calls=%async_computation.10 | async-start | bytes 4587520 | tf_op jit(solution)/shard_map/reduce_scatter | solution.py:109
  281.3 1.6 copy-start.5
  281.4 206.8 %reduce-scatter.14.cloned.1.call-start = ((), (), s32[]{:S(2)}) async-start(), calls=%async_computation.11 | async-start | bytes 4587520 | tf_op jit(solution)/shard_map/reduce_scatter | solution.py:113
Sparse Core Ops, SparseCore 0:
  63.0 116.6 reduce-scatter.7
  217.0 45.2 all-gather.1
  275.4 76.1 reduce-scatter.15
  354.5 43.3 reduce-scatter.9
  400.7 42.2 reduce-scatter.11
  445.8 42.2 reduce-scatter.13
